TPU v7x, 32 devices: a whole 2x2x4 slice. The times are simulated.
32 devices in a mesh: gy: 8 (over y, x, core), gz: 4 (over z).
Axes of the slice: x: 2, y: 2, z: 4, core: 2. Of those that a mesh axis runs over, the one named last changes fastest.
Arguments:
- initial_warmth: float32 [1024, 32, 512], P('gy', None, 'gz'), may hold values from -18 to 18
- transverse_factor: float32 [32, 512], P(None, 'gz'), may hold values from 0.05 to 0.24
- energy_supply_series: float32 [1024, 32, 512], P('gy', None, 'gz'), may hold values from -1.5 to 1.5
Outputs:
- temperature_next: float32 [1024, 32, 512], P('gy', None, 'gz')
All inputs are finite; a program needn't handle non-finite values.
Results may differ from a plain program's by a relative error of at most 0.0001.
Values sent between devices are 32-bit elements; how exact they have to be, the bound alone decides.
A program may use at most 64 MiB of HBM per device.

v0:
```python
import jax
import jax.numpy as jnp
import numpy as np
from jax import lax
from jax.sharding import PartitionSpec as P

ITERATION_TOTAL = 2


coupling = 400.0


def with_halo(block, sides, width):
    for axis, dim in sides:
        count = lax.axis_size(axis)
        forward = [(i, i + 1) for i in range(count - 1)]
        forward.append((count - 1, 0))
        backward = [(target, source) for source, target in forward]
        low = lax.ppermute(
            lax.slice_in_dim(block, block.shape[dim] - width, None, axis=dim), axis, forward
        )
        high = lax.ppermute(lax.slice_in_dim(block, 0, width, axis=dim), axis, backward)
        block = jnp.concatenate([low, block, high], axis=dim)
    return block


def circulant_table(length):
    decay_root = (1.0 + 2.0 * coupling - np.sqrt(1.0 + 4.0 * coupling)) / (2.0 * coupling)
    height = 1.0 / (1.0 + 2.0 * coupling - 2.0 * coupling * decay_root)
    spread = np.arange(length)
    column = (
        height * (decay_root**spread + decay_root ** (length - spread)) / (1.0 - decay_root**length)
    )
    offsets = (np.arange(length)[:, None] - np.arange(length)[None, :]) % length
    return jnp.asarray(column[offsets].astype(np.float32))


def solve_lines(lines):
    table = circulant_table(lines.shape[0])
    flat = lines.reshape(lines.shape[0], -1)
    solved = jnp.dot(
        table, flat, precision=lax.Precision.HIGHEST, preferred_element_type=jnp.float32
    )
    return solved.reshape(lines.shape)


def solve_pair(pair):
    return (solve_lines(pair[0]), pair[1])


def per_device(initial_warmth, transverse_factor, energy_supply_series):
    lines, source_lines = solve_pair(
        (
            lax.all_to_all(initial_warmth, "gy", split_axis=1, concat_axis=0, tiled=True),
            lax.all_to_all(energy_supply_series, "gy", split_axis=1, concat_axis=0, tiled=True),
        )
    )
    width_y = lines.shape[1]
    coefficient = lax.dynamic_slice_in_dim(
        transverse_factor, lax.axis_index("gy") * width_y, width_y, 0
    )
    for single_update in range(ITERATION_TOTAL):
        if single_update > 0:
            lines = solve_lines(lines)
        padded = with_halo(lines, (("gy", 1), ("gz", 2)), 1)
        second_difference = padded[:, 2:, 1:-1] + padded[:, :-2, 1:-1]
        second_difference = (
            second_difference + padded[:, 1:-1, 2:] + padded[:, 1:-1, :-2] - 4.0 * lines
        )
        lines = lines + coefficient[None] * second_difference + source_lines
    return lax.all_to_all(lines, "gy", split_axis=0, concat_axis=1, tiled=True)


def solution(mesh):
    placed = (P("gy", None, "gz"), P(None, "gz"), P("gy", None, "gz"))
    return jax.shard_map(
        per_device, mesh=mesh, in_specs=placed, out_specs=P("gy", None, "gz"), check_vma=False
    )
```

profile of v0, /device:TPU:0, one launch (start us, length us, event | category | flops | bytes accessed | tf_op | source)
XLA Modules:
  0.0 153.5 jit_solution(13330312396130296832)
XLA Ops:
  0.0 0.0 copy-start
  0.0 4.2 %copy.9 = f32[128,32,128]{2,0,1:T(8,128)} copy(f32[128,32,128]{2,1,0:T(8,128)} %param.5) | data formatting | bytes 4194304 | tf_op args[0]
  4.2 5.2 %all-to-all-start = ((f32[128,32,128]{2,0,1:T(8,128)}), f32[128,32,128]{2,0,1:T(8,128)S(1)}, u32[]{:S(2)}, u32[]{:S(2)}) async-start(f32[128,32,128]{2,0,1:T(8,128)} %copy.9), calls=%async_computation | async-start | bytes 4194304 | tf_op jit(solution)/shard_map/all_to_all | solution.py:54
  9.4 4.1 %copy.11 = f32[128,32,128]{2,0,1:T(8,128)} copy(f32[128,32,128]{2,1,0:T(8,128)} %param.7) | data formatting | bytes 4194304 | tf_op args[2]
  13.5 22.5 %all-to-all-done = f32[128,32,128]{2,0,1:T(8,128)S(1)} async-done(((f32[128,32,128]{2,0,1:T(8,128)}), f32[128,32,128]{2,0,1:T(8,128)S(1)}, u32[]{:S(2)}, u32[]{:S(2)}) %all-to-all-start) | async-done | bytes 2097184 | tf_op jit(solution)/shard_map/all_to_all | solution.py:54
  36.0 4.3 %all-to-all-start.1 = ((f32[128,32,128]{2,0,1:T(8,128)}), f32[128,32,128]{2,0,1:T(8,128)}, u32[]{:S(2)}, u32[]{:S(2)}) async-start(f32[128,32,128]{2,0,1:T(8,128)} %copy.11), calls=%async_computation.1 | async-start | bytes 4194304 | tf_op jit(solution)/shard_map/all_to_all | solution.py:55
  40.3 1.8 %copy.10 = f32[8,128,4,128]{1,0,3,2:T(8,128)} copy(f32[8,128,4,128]{3,1,2,0:T(8,128)S(1)} %bitcast.33) | data formatting | bytes 4194304 | tf_op jit(solution)/shard_map/all_to_all | solution.py:54
  42.2 0.0 copy-start.3
  42.2 2.2 %copy.17 = f32[64,8,8,128]{3,1,2,0:T(8,128)S(1)} copy(f32[64,8,8,128]{3,2,1,0:T(8,128)} %bitcast.34) | data formatting | bytes 4194304
  44.4 0.6 copy-done.3
  45.0 6.8 %fusion.16 = f32[1024,4,128]{0,2,1:T(8,128)S(1)} fusion(f32[1024,1024,1]{1,0,2:T(8,128)S(1)} %copy-done.3, f32[4,128,1024]{2,1,0:T(8,128)S(1)} %bitcast.37), kind=kOutput, calls=%fused_computation.40 | convolution fusion | flops 6442450944 | bytes 8388608 | tf_op jit(solution)/shard_map/dot_general | solution.py:41
  51.8 1.0 fusion.15
  52.9 2.5 %collective-permute-start = (f32[1024,1,128]{0,2,1:T(8,128)}, f32[1024,1,128]{0,2,1:T(8,128)S(1)}, u32[]{:S(2)}, u32[]{:S(2)}) collective-permute-start(f32[1024,1,128]{0,2,1:T(8,128)} %get-tuple-element.12), channel_id=1, source_target_pairs={{4,0},{8,4},{12,8},{16,12},{20,16},{24,20},{28,24},{0,28},{5,1},{9... | collective-permute-start | bytes 1572872 | tf_op jit(solution)/shard_map/ppermute | solution.py:22
  55.4 0.0 collective-permute-start.1
  55.4 19.8 %collective-permute-done = f32[1024,1,128]{0,2,1:T(8,128)S(1)} collective-permute-done((f32[1024,1,128]{0,2,1:T(8,128)}, f32[1024,1,128]{0,2,1:T(8,128)S(1)}, u32[]{:S(2)}, u32[]{:S(2)}) %collective-permute-start) | collective-permute-done | bytes 524320 | tf_op jit(solution)/shard_map/ppermute | solution.py:22
  75.2 2.3 %collective-permute-done.1 = f32[1024,1,128]{0,2,1:T(8,128)S(1)} collective-permute-done((f32[1024,1,128]{0,2,1:T(8,128)}, f32[1024,1,128]{0,2,1:T(8,128)S(1)}, u32[]{:S(2)}, u32[]{:S(2)}) %collective-permute-start.1) | collective-permute-done | bytes 524320 | tf_op jit(solution)/shard_map/ppermute | solution.py:19
  77.6 1.6 %collective-permute-start.3 = (f32[1024,6,1]{0,2,1:T(1,128)S(1)}, f32[1024,6,1]{0,2,1:T(1,128)S(1)}, u32[]{:S(2)}, u32[]{:S(2)}) collective-permute-start(f32[1024,6,1]{0,2,1:T(1,128)S(1)} %get-tuple-element.8), channel_id=1, source_target_pairs={{0,1},{1,2},{2,3},{3,0},{4,5},{5,6},{6,7},{7,4},{8,9},{9,10},{10,1... | collective-permute-start | bytes 73736 | tf_op jit(solution)/shard_map/ppermute | solution.py:19
  79.2 2.3 %collective-permute-start.2 = (f32[1024,6,1]{0,2,1:T(1,128)S(1)}, f32[1024,6,1]{0,2,1:T(1,128)S(1)}, u32[]{:S(2)}, u32[]{:S(2)}) collective-permute-start(f32[1024,6,1]{0,2,1:T(1,128)S(1)} %get-tuple-element.7), channel_id=1, source_target_pairs={{1,0},{2,1},{3,2},{0,3},{5,4},{6,5},{7,6},{4,7},{9,8},{10,9},{11,1... | collective-permute-start | bytes 73736 | tf_op jit(solution)/shard_map/ppermute | solution.py:22
  81.5 0.0 copy-done
  81.5 0.0 all-to-all-done.1
  81.5 2.9 %copy.12 = f32[128,8,4,128]{0,1,3,2:T(8,128)} copy(f32[128,8,4,128]{3,0,2,1:T(8,128)} %bitcast.5) | data formatting | bytes 4194304 | tf_op jit(solution)/shard_map/all_to_all | solution.py:55
  84.4 2.7 %all_to_all.43 = f32[1024,4,128]{0,2,1:T(8,128)} reshape(f32[8,128,4,128]{1,0,3,2:T(8,128)} %bitcast.35) | data formatting | bytes 4194304 | tf_op jit(solution)/shard_map/all_to_all | solution.py:55
  87.1 0.0 copy-start.2
  87.1 0.0 collective-permute-done.3
  87.1 0.0 collective-permute-done.2
  87.1 3.3 %fusion.11 = f32[1024,4,128]{0,2,1:T(8,128)S(1)} fusion(f32[1024,4,128]{0,2,1:T(8,128)} %all_to_all.43, f32[1024,4,128]{0,2,1:T(8,128)S(1)} %fusion.16, f32[1024,6,1]{0,2,1:T(1,128)S(1)} %collective-permute-done.3, f32[1024,1,128]{0,2,1:T(8,128)S(1)} %collective-permute-done, f32[1024,1,128]{0,2,1:T(8,128)S(1)} %collective-permute-done.1, ...), kind=kLoop, calls=%fused_computation.21 | loop fusion | flops 8388608 | bytes 7391232 | tf_op jit(solution)/shard_map/add | solution.py:70
  90.4 0.0 copy-done.2
  90.4 6.8 %fusion.17 = f32[1024,512]{0,1:T(8,128)S(1)} fusion(f32[1024,1024]{1,0:T(8,128)S(1)} %copy-done.2, f32[1024,512]{0,1:T(8,128)S(1)} %bitcast.38), kind=kOutput, calls=%fused_computation.41 | convolution fusion | flops 6442450944 | bytes 8388608 | tf_op jit(solution)/shard_map/dot_general | solution.py:41
  97.2 0.1 fusion.14
  97.3 0.0 copy-start.1
  97.3 0.2 collective-permute-start.4
  97.5 0.4 collective-permute-start.5
  97.9 11.5 %collective-permute-done.4 = f32[1024,1,128]{0,2,1:T(8,128)S(1)} collective-permute-done((f32[1024,1,128]{0,2,1:T(8,128)S(1)}, f32[1024,1,128]{0,2,1:T(8,128)S(1)}, u32[]{:S(2)}, u32[]{:S(2)}) %collective-permute-start.4) | collective-permute-done | bytes 524320 | tf_op jit(solution)/shard_map/ppermute | solution.py:22
  109.4 2.5 %collective-permute-done.5 = f32[1024,1,128]{0,2,1:T(8,128)S(1)} collective-permute-done((f32[1024,1,128]{0,2,1:T(8,128)S(1)}, f32[1024,1,128]{0,2,1:T(8,128)S(1)}, u32[]{:S(2)}, u32[]{:S(2)}) %collective-permute-start.5) | collective-permute-done | bytes 524320 | tf_op jit(solution)/shard_map/ppermute | solution.py:19
  111.9 0.1 collective-permute-start.7
  112.0 3.8 %collective-permute-start.6 = (f32[1024,6,1]{0,2,1:T(1,128)S(1)}, f32[1024,6,1]{0,2,1:T(1,128)S(1)}, u32[]{:S(2)}, u32[]{:S(2)}) collective-permute-start(f32[1024,6,1]{0,2,1:T(1,128)S(1)} %get-tuple-element.5), channel_id=1, source_target_pairs={{1,0},{2,1},{3,2},{0,3},{5,4},{6,5},{7,6},{4,7},{9,8},{10,9},{11,1... | collective-permute-start | bytes 73736 | tf_op jit(solution)/shard_map/ppermute | solution.py:22
  115.8 1.8 %collective-permute-done.7 = f32[1024,6,1]{0,2,1:T(1,128)S(1)} collective-permute-done((f32[1024,6,1]{0,2,1:T(1,128)S(1)}, f32[1024,6,1]{0,2,1:T(1,128)S(1)}, u32[]{:S(2)}, u32[]{:S(2)}) %collective-permute-start.7) | collective-permute-done | bytes 24608 | tf_op jit(solution)/shard_map/ppermute | solution.py:19
  117.6 0.0 collective-permute-done.6
  117.6 0.0 copy-done.1
  117.6 2.9 %fusion.4 = f32[1024,4,128]{0,2,1:T(8,128)} fusion(f32[1024,4,128]{0,2,1:T(8,128)S(1)} %copy-done.1, f32[1024,4,128]{0,2,1:T(8,128)S(1)} %bitcast.32, f32[1024,6,1]{0,2,1:T(1,128)S(1)} %collective-permute-done.7, f32[1024,1,128]{0,2,1:T(8,128)S(1)} %collective-permute-done.4, f32[1024,1,128]{0,2,1:T(8,128)S(1)} %collective-permute-done.5, ...), kind=kLoop, calls=%fused_computation.6 | loop fusion | flops 8388608 | bytes 7391232 | tf_op jit(solution)/shard_map/add | solution.py:70
  120.5 2.0 %copy.13 = f32[1024,4,128]{2,1,0:T(4,128)S(1)} copy(f32[1024,4,128]{0,2,1:T(8,128)} %fusion.4) | data formatting | bytes 4194304 | tf_op jit(solution)/shard_map/add | solution.py:70
  122.5 29.1 %all_to_all.51 = f32[1024,4,128]{2,1,0:T(4,128)S(1)} all-to-all(f32[1024,4,128]{2,1,0:T(4,128)S(1)} %copy.13), channel_id=1, replica_groups=mesh['gy'=8,'gz'=4] {'gy'}, dimensions={0} | all-to-all | bytes 4194304 | tf_op jit(solution)/shard_map/all_to_all | solution.py:71
  151.6 1.9 %copy.14 = f32[128,8,4,128]{3,2,1,0:T(4,128)} copy(f32[128,8,4,128]{3,2,0,1:T(4,128)S(1)} %bitcast.36) | data formatting | bytes 4194304 | tf_op jit(solution)/shard_map/all_to_all | solution.py:71
  (3 shorter events, 0.1 us)
Async XLA Ops:
  0.0 81.5 %copy-start = (f32[32,128]{1,0:T(8,128)S(1)}, f32[32,128]{1,0:T(8,128)}, u32[]{:S(2)}) copy-start(f32[32,128]{1,0:T(8,128)} %param.6) | copy-start | bytes 49156
  4.2 31.8 %all-to-all-start = ((f32[128,32,128]{2,0,1:T(8,128)}), f32[128,32,128]{2,0,1:T(8,128)S(1)}, u32[]{:S(2)}, u32[]{:S(2)}) async-start(f32[128,32,128]{2,0,1:T(8,128)} %copy.9), calls=%async_computation | async-start | bytes 4194304 | tf_op jit(solution)/shard_map/all_to_all | solution.py:54
  36.0 45.5 %all-to-all-start.1 = ((f32[128,32,128]{2,0,1:T(8,128)}), f32[128,32,128]{2,0,1:T(8,128)}, u32[]{:S(2)}, u32[]{:S(2)}) async-start(f32[128,32,128]{2,0,1:T(8,128)} %copy.11), calls=%async_computation.1 | async-start | bytes 4194304 | tf_op jit(solution)/shard_map/all_to_all | solution.py:55
  42.2 2.8 %copy-start.3 = (f32[1024,1024,1]{1,0,2:T(8,128)S(1)}, f32[1024,1024,1]{1,0,2:T(8,128)}, u32[]{:S(2)}) copy-start(f32[1024,1024,1]{1,0,2:T(8,128)} %constant.17) | copy-start | bytes 12582916
  52.9 22.3 %collective-permute-start = (f32[1024,1,128]{0,2,1:T(8,128)}, f32[1024,1,128]{0,2,1:T(8,128)S(1)}, u32[]{:S(2)}, u32[]{:S(2)}) collective-permute-start(f32[1024,1,128]{0,2,1:T(8,128)} %get-tuple-element.12), channel_id=1, source_target_pairs={{4,0},{8,4},{12,8},{16,12},{20,16},{24,20},{28,24},{0,28},{5,1},{9... | collective-permute-start | bytes 1572872 | tf_op jit(solution)/shard_map/ppermute | solution.py:22
  55.4 22.1 %collective-permute-start.1 = (f32[1024,1,128]{0,2,1:T(8,128)}, f32[1024,1,128]{0,2,1:T(8,128)S(1)}, u32[]{:S(2)}, u32[]{:S(2)}) collective-permute-start(f32[1024,1,128]{0,2,1:T(8,128)} %get-tuple-element.11), channel_id=1, source_target_pairs={{0,4},{4,8},{8,12},{12,16},{16,20},{20,24},{24,28},{28,0},{1,5},{5... | collective-permute-start | bytes 1572872 | tf_op jit(solution)/shard_map/ppermute | solution.py:19
  77.6 9.5 %collective-permute-start.3 = (f32[1024,6,1]{0,2,1:T(1,128)S(1)}, f32[1024,6,1]{0,2,1:T(1,128)S(1)}, u32[]{:S(2)}, u32[]{:S(2)}) collective-permute-start(f32[1024,6,1]{0,2,1:T(1,128)S(1)} %get-tuple-element.8), channel_id=1, source_target_pairs={{0,1},{1,2},{2,3},{3,0},{4,5},{5,6},{6,7},{7,4},{8,9},{9,10},{10,1... | collective-permute-start | bytes 73736 | tf_op jit(solution)/shard_map/ppermute | solution.py:19
  79.2 7.9 %collective-permute-start.2 = (f32[1024,6,1]{0,2,1:T(1,128)S(1)}, f32[1024,6,1]{0,2,1:T(1,128)S(1)}, u32[]{:S(2)}, u32[]{:S(2)}) collective-permute-start(f32[1024,6,1]{0,2,1:T(1,128)S(1)} %get-tuple-element.7), channel_id=1, source_target_pairs={{1,0},{2,1},{3,2},{0,3},{5,4},{6,5},{7,6},{4,7},{9,8},{10,9},{11,1... | collective-permute-start | bytes 73736 | tf_op jit(solution)/shard_map/ppermute | solution.py:22
  87.1 3.3 %copy-start.2 = (f32[1024,1024]{1,0:T(8,128)S(1)}, f32[1024,1024]{1,0:T(8,128)}, u32[]{:S(2)}) copy-start(f32[1024,1024]{1,0:T(8,128)} %constant.16.clone) | copy-start | bytes 12582916
  97.3 20.3 %copy-start.1 = (f32[1024,4,128]{0,2,1:T(8,128)S(1)}, f32[1024,4,128]{0,2,1:T(8,128)}, u32[]{:S(2)}) copy-start(f32[1024,4,128]{0,2,1:T(8,128)} %all_to_all.43) | copy-start | bytes 6291460
  97.3 12.1 %collective-permute-start.4 = (f32[1024,1,128]{0,2,1:T(8,128)S(1)}, f32[1024,1,128]{0,2,1:T(8,128)S(1)}, u32[]{:S(2)}, u32[]{:S(2)}) collective-permute-start(f32[1024,1,128]{0,2,1:T(8,128)S(1)} %get-tuple-element.10), channel_id=1, source_target_pairs={{4,0},{8,4},{12,8},{16,12},{20,16},{24,20},{28,24},{0,28},{5,1},{9... | collective-permute-start | bytes 1572872 | tf_op jit(solution)/shard_map/ppermute | solution.py:22
  97.5 14.4 %collective-permute-start.5 = (f32[1024,1,128]{0,2,1:T(8,128)S(1)}, f32[1024,1,128]{0,2,1:T(8,128)S(1)}, u32[]{:S(2)}, u32[]{:S(2)}) collective-permute-start(f32[1024,1,128]{0,2,1:T(8,128)S(1)} %get-tuple-element.9), channel_id=1, source_target_pairs={{0,4},{4,8},{8,12},{12,16},{16,20},{20,24},{24,28},{28,0},{1,5},{5... | collective-permute-start | bytes 1572872 | tf_op jit(solution)/shard_map/ppermute | solution.py:19
  111.9 5.7 %collective-permute-start.7 = (f32[1024,6,1]{0,2,1:T(1,128)S(1)}, f32[1024,6,1]{0,2,1:T(1,128)S(1)}, u32[]{:S(2)}, u32[]{:S(2)}) collective-permute-start(f32[1024,6,1]{0,2,1:T(1,128)S(1)} %get-tuple-element.6), channel_id=1, source_target_pairs={{0,1},{1,2},{2,3},{3,0},{4,5},{5,6},{6,7},{7,4},{8,9},{9,10},{10,1... | collective-permute-start | bytes 73736 | tf_op jit(solution)/shard_map/ppermute | solution.py:19
  112.0 5.6 %collective-permute-start.6 = (f32[1024,6,1]{0,2,1:T(1,128)S(1)}, f32[1024,6,1]{0,2,1:T(1,128)S(1)}, u32[]{:S(2)}, u32[]{:S(2)}) collective-permute-start(f32[1024,6,1]{0,2,1:T(1,128)S(1)} %get-tuple-element.5), channel_id=1, source_target_pairs={{1,0},{2,1},{3,2},{0,3},{5,4},{6,5},{7,6},{4,7},{9,8},{10,9},{11,1... | collective-permute-start | bytes 73736 | tf_op jit(solution)/shard_map/ppermute | solution.py:22
where the time goes:
time: 154 us
  waiting for transfers between devices  60.4 us (39%)
  blocking collectives  29.1 us (19%)
  local copies, waits for them, and re-layouts  23.7 us (15%)
  starting transfers between devices  20.4 us (13%)
  matrix products  13.6 us (9%)
  other arithmetic  6.27 us (4%)
    ppermute x4, waiting for transfers between devices, with_halo(): lax.ppermute(lax.slice_in_dim(block, 0, width, axis=dim), axis, backward)  31.3 us
    all_to_all x1, blocking collectives, per_device(): return lax.all_to_all(lines, 'gy', split_axis=0, concat_axis=1, tiled=True)  29.1 us
    all_to_all x1, waiting for transfers between devices, per_device(): lax.all_to_all(initial_warmth, 'gy', split_axis=1, concat_axis=0, tiled=T...  22.5 us
    dot_general x2, matrix products, solve_lines(): jnp.dot(table, flat, precision=lax.Precision.HIGHEST, preferred_element_t...  13.6 us
    unnamed x11, local copies, waits for them, and re-layouts  11.1 us
    ppermute x4, starting transfers between devices, with_halo(): lax.ppermute(lax.slice_in_dim(block, 0, width, axis=dim), axis, backward)  8.8 us
    ppermute x4, waiting for transfers between devices, with_halo(): lax.ppermute(lax.slice_in_dim(block, block.shape[dim] - width, None, axis...  6.62 us
    add x2, other arithmetic, per_device(): lines = lines + coefficient[None] * second_difference + source_lines  6.2 us
  transfers between devices with their start and end apart: 10, of which 6 were waited for; matrix products, arithmetic and copies ran while one was open for 12% of the time, Pallas kernels for 0%

commit v1 on v0

v1 whole, which is shorter than its diff:
```python
import jax
import jax.numpy as jnp
import numpy as np
from jax import lax
from jax.sharding import PartitionSpec as P

coupling = 400.0


def tables(m, parts):
    root = (1.0 + 2.0 * coupling - np.sqrt(1.0 + 4.0 * coupling)) / (2.0 * coupling)
    height = 1.0 / (1.0 + 2.0 * coupling - 2.0 * coupling * root)
    delta = (1.0 + root**2) / (1.0 - root**2)
    cell = np.arange(m)
    distance = np.abs(cell[:, None] - cell[None, :])
    local = np.concatenate(
        [height**2 * (delta + distance) * root**distance, height * root**distance], axis=1
    )
    rows = []
    for reach in (m - 1 - cell, cell):
        fall = root**reach
        rows.append(np.concatenate([height**2 * fall, 0.0 * fall]))
        rows.append(np.concatenate([height**2 * (delta + reach) * fall, height * fall]))
    sums = np.stack(rows)
    step = root**m
    whole = step**parts
    mix = np.zeros((parts, 4, parts, 4))
    for d in range(parts):
        for p in range(1, parts + 1):
            near = step ** (p - 1) / (1.0 - whole)
            far = m * step ** (p - 1) * (
                (p - 1) / (1.0 - whole) + parts * whole / (1.0 - whole) ** 2
            )
            for first, other in ((0, (d - p) % parts), (2, (d + p) % parts)):
                mix[d, first, other, first] = near
                mix[d, first + 1, other, first + 1] = near
                mix[d, first + 1, other, first] = far
    columns = []
    for reach in (cell + 1, m - cell):
        columns += [reach * root**reach, root**reach]
    spread = np.stack(columns, axis=1)
    return [t.astype(np.float32) for t in (local, sums, mix, spread)]


def shifted(block, axis, by):
    count = lax.axis_size(axis)
    return lax.ppermute(block, axis, [(i, (i + by) % count) for i in range(count)])


def transverse(wide, c):
    mid = wide[..., 1:-1]
    around = jnp.roll(mid, 1, -2) + jnp.roll(mid, -1, -2) + wide[..., 2:] + wide[..., :-2]
    return mid + c * (around - 4.0 * mid)


def per_device(field, c, q):
    m, ny, nz = field.shape
    parts = lax.axis_size("gy")
    local, sums, mix, spread = tables(m, parts)

    def edges(a, b, at):
        planes = [field[:, :, a], field[:, :, b], q[:, :, at]]
        return jnp.concatenate(planes + [c[None, :, at]], axis=0)

    low = shifted(edges(nz - 2, nz - 1, nz - 1), "gz", 1)
    high = shifted(edges(1, 0, 0), "gz", -1)

    def plane(packed, k):
        return packed[k * m : (k + 1) * m, :, None]

    wide_field = jnp.concatenate(
        [plane(low, 0), plane(low, 1), field, plane(high, 1), plane(high, 0)], axis=2
    )
    wide_q = jnp.concatenate([plane(low, 2), q, plane(high, 2)], axis=2)
    wide_c = jnp.concatenate([low[3 * m, :, None], c, high[3 * m, :, None]], axis=1)
    g = transverse(transverse(wide_field, wide_c), c)
    h = transverse(wide_q, c)
    both = jnp.concatenate([g, h], axis=0)

    def dot(a, b):
        return lax.dot_general(
            a, b, (((1,), (0,)), ((), ())), precision=lax.Precision.HIGH,
            preferred_element_type=jnp.float32,
        )

    planes = dot(jnp.asarray(sums), both)
    gathered = lax.all_gather(planes, "gy", axis=0, tiled=True)
    mine = lax.dynamic_index_in_dim(
        jnp.asarray(mix.reshape(parts, 4, parts * 4)), lax.axis_index("gy"), 0, False
    )
    incoming = dot(mine, gathered)
    return dot(jnp.asarray(local), both) + dot(jnp.asarray(spread), incoming) + q


def solution(mesh):
    placed = (P("gy", None, "gz"), P(None, "gz"), P("gy", None, "gz"))
    return jax.shard_map(
        per_device, mesh=mesh, in_specs=placed, out_specs=P("gy", None, "gz"), check_vma=False
    )
```

time: 154 us -> 72 us (0.47)
  waiting for transfers between devices: 60.4 us -> 0.01 us
  local copies, waits for them, and re-layouts: 23.7 us -> 43.3 us
  blocking collectives: 29.1 us -> 10.2 us
  starting transfers between devices: 20.4 us -> 5.36 us
  matrix products: 13.6 us -> 6.71 us
    ppermute x8 -> x2, waiting for transfers between devices: 37.9 us -> 0.01 us  [shifted(): lax.ppermute(block, axis, [(i, (i + by) % count) for i in range(count)])]
    all_to_all x1 -> x0, blocking collectives: 29.1 us -> none  [per_device(): return lax.all_to_all(lines, 'gy', split_axis=0, concat_axis=1, tiled=True)]
    all_to_all x2 -> x0, waiting for transfers between devices: 22.5 us -> none  [the longest x1 22.5 us: per_device(): lax.all_to_all(initial_warmth, 'gy', split_axis=1, concat_axis=0, tiled=T...]
    slice x2 -> x10, local copies, waits for them, and re-layouts: 1.14 us -> 18 us  [the longest x2 11.5 us: edges(): planes = [field[:, :, a], field[:, :, b], q[:, :, at]]]
    unnamed x11 -> x28, local copies, waits for them, and re-layouts: 11.1 us -> 23.3 us
    all_gather x0 -> x1, blocking collectives: none -> 10.2 us  [per_device(): gathered = lax.all_gather(planes, 'gy', axis=0, tiled=True)]
    all_to_all x2 -> x0, starting transfers between devices: 9.54 us -> none  [the longest x1 5.2 us: per_device(): lax.all_to_all(initial_warmth, 'gy', split_axis=1, concat_axis=0, tiled=T...]
    all_to_all x4 -> x0, local copies, waits for them, and re-layouts: 9.38 us -> none  [the longest x2 5.62 us: per_device(): lax.all_to_all(energy_supply_series, 'gy', split_axis=1, concat_axis=0, t...]
  transfers between devices with their start and end apart: 10 -> 2, of which waited for: 6 -> 0; matrix products, arithmetic and copies ran while one was open for 12% -> 24% of each run, Pallas kernels for 0% -> 0%
where the time goes in v1:
time: 72 us; the launch traced here: 71.5 us
  local copies, waits for them, and re-layouts  43.3 us (60%)
  blocking collectives  10.2 us (14%)
  matrix products  6.71 us (9%)
  other arithmetic  5.76 us (8%)
  starting transfers between devices  5.36 us (7%)
    unnamed x28, local copies, waits for them, and re-layouts  23.3 us
    slice x2, local copies, waits for them, and re-layouts, edges(): planes = [field[:, :, a], field[:, :, b], q[:, :, at]]  11.5 us
    all_gather x1, blocking collectives, per_device(): gathered = lax.all_gather(planes, 'gy', axis=0, tiled=True)  10.2 us
    dot_general x4, matrix products, dot(): lax.dot_general(a, b, (((1,), (0,)), ((), ())), precision=lax.Precision.H...  6.71 us
    slice x6, local copies, waits for them, and re-layouts, transverse(): jnp.roll(mid, -1, -2)  6.49 us
    ppermute x2, starting transfers between devices, shifted(): lax.ppermute(block, axis, [(i, (i + by) % count) for i in range(count)])  5.36 us
    add x2, other arithmetic, transverse(): return mid + c * (around - 4.0 * mid)  3.89 us
    add x1, local copies, waits for them, and re-layouts, per_device(): dot(jnp.asarray(local), both) + dot(jnp.asarray(spread), incoming) + q  1.97 us
  transfers between devices with their start and end apart: 2, of which 0 were waited for; matrix products, arithmetic and copies ran while one was open for 24% of the time, Pallas kernels for 0%

profile of v1, /device:TPU:0, one launch (start us, length us, event | category | flops | bytes accessed | tf_op | source)
XLA Modules:
  0.0 71.5 jit_solution(9735770621171226381)
XLA Ops:
  0.0 8.7 %fusion.28 = (f32[128,32,1]{2,1,0:T(8,128)}, f32[128,32,1]{2,1,0:T(8,128)}, f32[128,32,1]{2,1,0:T(8,128)}, f32[128,32,1]{2,1,0:T(8,128)}) fusion(f32[128,32,128]{2,1,0:T(8,128)} %param.7), kind=kLoop, calls=%fused_computation.45 | loop fusion | bytes 131072 | tf_op jit(solution)/shard_map/slice | solution.py:62
  8.7 0.0 copy-start.2
  8.7 2.8 %copy.96 = f32[128,32,1]{0,1,2:T(8,128)S(1)} copy(f32[128,32,1]{2,1,0:T(8,128)} %get-tuple-element.19) | data formatting | bytes 32768
  11.5 2.7 %copy.97 = f32[128,32,1]{0,1,2:T(8,128)S(1)} copy(f32[128,32,1]{2,1,0:T(8,128)} %get-tuple-element.18) | data formatting | bytes 32768
  14.2 0.0 copy-done.2
  14.2 2.8 %fusion.29 = (f32[128,32,1]{2,1,0:T(8,128)}, f32[128,32,1]{2,1,0:T(8,128)}) fusion(f32[128,32,128]{2,1,0:T(8,128)S(1)} %copy-done.2), kind=kLoop, calls=%fused_computation.46 | loop fusion | bytes 65536 | tf_op jit(solution)/shard_map/slice | solution.py:62
  16.9 0.0 copy-start.6
  16.9 2.7 %copy.98 = f32[128,32,1]{0,1,2:T(8,128)S(1)} copy(f32[128,32,1]{2,1,0:T(8,128)} %get-tuple-element.22) | data formatting | bytes 32768
  19.6 0.0 copy-done.6
  19.6 0.1 slice_bitcast_fusion.2
  19.7 3.1 %collective-permute-start = (f32[385,32]{0,1:T(8,128)S(1)}, f32[385,32]{0,1:T(8,128)S(1)}, u32[]{:S(2)}, u32[]{:S(2)}) collective-permute-start(f32[385,32]{0,1:T(8,128)S(1)} %pad_maximum_fusion.8), channel_id=1, source_target_pairs={{0,1},{1,2},{2,3},{3,0},{4,5},{5,6},{6,7},{7,4},{8,9},{9,10},{10,1... | collective-permute-start | bytes 147848 | tf_op jit(solution)/shard_map/ppermute | solution.py:47
  22.8 2.7 %copy.99 = f32[128,32,1]{0,1,2:T(8,128)S(1)} copy(f32[128,32,1]{2,1,0:T(8,128)} %get-tuple-element.17) | data formatting | bytes 32768
  25.4 2.7 %copy.100 = f32[128,32,1]{0,1,2:T(8,128)S(1)} copy(f32[128,32,1]{2,1,0:T(8,128)} %get-tuple-element.20) | data formatting | bytes 32768
  28.1 2.7 %copy.101 = f32[128,32,1]{0,1,2:T(8,128)S(1)} copy(f32[128,32,1]{2,1,0:T(8,128)} %get-tuple-element.21) | data formatting | bytes 32768
  30.7 2.3 %collective-permute-start.1 = (f32[385,32]{0,1:T(8,128)S(1)}, f32[385,32]{0,1:T(8,128)S(1)}, u32[]{:S(2)}, u32[]{:S(2)}) collective-permute-start(f32[385,32]{0,1:T(8,128)S(1)} %pad_maximum_fusion.9), channel_id=1, source_target_pairs={{0,3},{1,0},{2,1},{3,2},{4,7},{5,4},{6,5},{7,6},{8,11},{9,8},{10,9... | collective-permute-start | bytes 147848 | tf_op jit(solution)/shard_map/ppermute | solution.py:47
  33.0 1.9 %copy.89 = f32[128,32,128]{0,2,1:T(8,128)} copy(f32[128,32,128]{2,1,0:T(8,128)S(1)} %copy-done.2) | data formatting | bytes 4194304 | tf_op args[2]
  34.9 0.0 copy-start
  34.9 4.8 %fusion.26 = (f32[128,31,128]{0,2,1:T(8,128)}, f32[128,31,128]{0,2,1:T(8,128)}) fusion(f32[128,32,128]{0,2,1:T(8,128)} %copy.89), kind=kLoop, calls=%fused_computation.43 | loop fusion | bytes 8126464 | tf_op jit(solution)/shard_map/jit(_roll_static)/slice | solution.py:52
  39.7 0.9 %fusion.27 = (f32[128,1,128]{0,2,1:T(8,128)S(1)}, f32[128,1,128]{0,2,1:T(8,128)S(1)}) fusion(f32[128,32,128]{0,2,1:T(8,128)} %copy.89), kind=kLoop, calls=%fused_computation.44 | loop fusion | bytes 262144 | tf_op jit(solution)/shard_map/jit(_roll_static)/slice | solution.py:52
  40.6 0.0 copy-done
  40.6 1.9 %copy.72 = f32[128,32,128]{0,2,1:T(8,128)} copy(f32[128,32,128]{2,1,0:T(8,128)S(1)} %copy-done) | data formatting | bytes 4194304 | tf_op args[0]
  42.4 0.0 collective-permute-done
  42.4 0.0 collective-permute-done.1
  42.5 1.8 %pad_maximum_fusion.3 = f32[128,32,130]{0,2,1:T(8,128)S(1)} fusion(f32[128,32,1]{0,2,1:T(1,128)S(1)} %bitcast.44, f32[128,32,128]{0,2,1:T(8,128)} %copy.72, f32[128,32,1]{0,2,1:T(1,128)S(1)} %bitcast.42), kind=kLoop, calls=%fused_computation.3 | loop fusion | flops 1064960 | bytes 4259840 | tf_op jit(solution)/shard_map/concatenate | solution.py:71
  44.3 0.0 copy-start.3
  44.3 0.3 fusion.24
  44.6 0.1 pad_maximum_fusion.10
  44.7 1.2 %copy-done.3 = f32[128,32,128]{0,2,1:T(8,128)S(1)} copy-done((f32[128,32,128]{0,2,1:T(8,128)S(1)}, f32[128,32,128]{0,2,1:T(8,128)}, u32[]{:S(2)}) %copy-start.3) | copy-done | bytes 2097176
  45.8 1.5 %fusion.6 = f32[128,32,130]{0,2,1:T(8,128)S(1)} fusion(f32[128,31,130]{0,2,1:T(8,128)S(1)} %get-tuple-element.10, f32[128,1,130]{0,2,1:T(8,128)S(1)} %get-tuple-element.12, f32[128,1,130]{0,2,1:T(8,128)S(1)} %get-tuple-element.11, f32[128,31,130]{0,2,1:T(8,128)S(1)} %get-tuple-element.9, f32[128,32,1]{0,2,1:T(1,128)S(1)} %bitcast.47, ...), kind=kLoop, calls=%fused_computation.9 | loop fusion | flops 7987200 | bytes 8569088 | tf_op jit(solution)/shard_map/add | solution.py:53
  47.4 0.0 copy-start.1
  47.4 0.0 copy-start.4
  47.4 0.0 copy-start.5
  47.4 0.5 fusion.22
  47.9 1.0 %copy-done.1 = f32[128,32,128]{0,2,1:T(8,128)S(1)} copy-done((f32[128,32,128]{0,2,1:T(8,128)S(1)}, f32[128,32,128]{0,2,1:T(8,128)}, u32[]{:S(2)}) %copy-start.1) | copy-done | bytes 2097176
  49.0 0.6 copy-done.4
  49.6 0.6 copy-done.5
  50.2 0.0 copy-start.8
  50.2 2.4 %fusion.14 = (f32[128,32,128]{0,2,1:T(8,128)S(1)}, f32[128,32,128]{0,2,1:T(8,128)S(1)}) fusion(f32[128,32,130]{0,2,1:T(8,128)S(1)} %fusion.6, f32[128,31,128]{0,2,1:T(8,128)S(1)} %get-tuple-element.6, f32[128,1,128]{0,2,1:T(8,128)S(1)} %get-tuple-element.8, f32[128,1,128]{0,2,1:T(8,128)S(1)} %get-tuple-element.7, f32[128,31,128]{0,2,1:T(8,128)S(1)} %get-tuple-element.5, ...), kind=kLoop, calls=%fused_computation.20 | loop fusion | flops 10485760 | bytes 21020672 | tf_op jit(solution)/shard_map/add | solution.py:53
  52.6 0.0 copy-done.8
  52.6 0.0 copy-start.9
  52.6 1.8 %fusion = f32[4,32,128]{2,0,1:T(4,128)S(1)} fusion(f32[4,256,1]{1,0,2:T(4,128)S(1)} %copy-done.8, f32[128,32,128]{0,2,1:T(8,128)S(1)} %get-tuple-element.30, f32[128,32,128]{0,2,1:T(8,128)S(1)} %get-tuple-element.29), kind=kOutput, calls=%fused_computation.1 | convolution fusion | flops 26214400 | bytes 4263936 | tf_op jit(solution)/shard_map/dot_general | solution.py:81
  54.4 0.0 copy-start.7
  54.4 10.2 %all_gather.3 = f32[32,32,128]{2,1,0:T(8,128)S(1)} all-gather(f32[4,32,128]{2,1,0:T(8,128)S(1)} %copy.91), channel_id=1, replica_groups=mesh['gy'=8,'gz'=4] {'gy'}, dimensions={0}, use_global_device_ids=true | all-gather | bytes 589824 | tf_op jit(solution)/shard_map/all_gather | solution.py:87
  64.6 1.2 %fusion.15 = f32[4,32,128]{2,0,1:T(4,128)S(1)} fusion(f32[32,32,128]{2,1,0:T(8,128)S(1)} %all_gather.3, f32[8,4,32]{2,1,0:T(4,128)} %constant.24.clone, s32[]{:T(128)S(6)} %select_n.4), kind=kOutput, calls=%fused_computation.25 | convolution fusion | flops 3145728 | bytes 591876 | tf_op jit(solution)/shard_map/dot_general | solution.py:81
  65.8 0.0 copy-done.9
  65.8 1.8 %fusion.32 = f32[32,128,128]{2,1,0:T(8,128)S(1)} fusion(f32[4,32,128]{2,0,1:T(4,128)S(1)} %fusion.15, f32[128,4,1]{0,1,2:T(4,128)S(1)} %copy-done.9), kind=kOutput, calls=%fused_computation.49 | convolution fusion | flops 12582912 | bytes 2164736 | tf_op jit(solution)/shard_map/dot_general | solution.py:81
  67.7 0.0 copy-done.7
  67.7 1.9 %bitcast_add_fusion = f32[128,32,128]{0,2,1:T(8,128)S(1)} fusion(f32[128,32,128]{0,2,1:T(8,128)S(1)} %copy-done.1, f32[32,128,128]{2,1,0:T(8,128)S(1)} %fusion.32, f32[128,256,1]{1,0,2:T(8,128)S(1)} %copy-done.7, f32[128,32,128]{0,2,1:T(8,128)S(1)} %get-tuple-element.30, f32[128,32,128]{0,2,1:T(8,128)S(1)} %get-tuple-element.29), kind=kOutput, calls=%fused_computation.24 | convolution fusion | flops 807403520 | bytes 10616832 | tf_op jit(solution)/shard_map/dot_general | solution.py:81
  69.6 2.0 %copy.94 = f32[128,32,128]{2,1,0:T(8,128)} copy(f32[128,32,128]{0,2,1:T(8,128)S(1)} %bitcast_add_fusion) | data formatting | bytes 4194304 | tf_op jit(solution)/shard_map/add | solution.py:92
  (9 shorter events, 0.1 us)
Async XLA Ops:
  8.7 5.5 %copy-start.2 = (f32[128,32,128]{2,1,0:T(8,128)S(1)}, f32[128,32,128]{2,1,0:T(8,128)}, u32[]{:S(2)}) copy-start(f32[128,32,128]{2,1,0:T(8,128)} %param.9) | copy-start | bytes 6291460
  16.9 2.7 %copy-start.6 = (f32[32,128]{1,0:T(8,128)S(1)}, f32[32,128]{1,0:T(8,128)}, u32[]{:S(2)}) copy-start(f32[32,128]{1,0:T(8,128)} %param.8) | copy-start | bytes 49156
  19.7 22.8 %collective-permute-start = (f32[385,32]{0,1:T(8,128)S(1)}, f32[385,32]{0,1:T(8,128)S(1)}, u32[]{:S(2)}, u32[]{:S(2)}) collective-permute-start(f32[385,32]{0,1:T(8,128)S(1)} %pad_maximum_fusion.8), channel_id=1, source_target_pairs={{0,1},{1,2},{2,3},{3,0},{4,5},{5,6},{6,7},{7,4},{8,9},{9,10},{10,1... | collective-permute-start | bytes 147848 | tf_op jit(solution)/shard_map/ppermute | solution.py:47
  30.7 11.7 %collective-permute-start.1 = (f32[385,32]{0,1:T(8,128)S(1)}, f32[385,32]{0,1:T(8,128)S(1)}, u32[]{:S(2)}, u32[]{:S(2)}) collective-permute-start(f32[385,32]{0,1:T(8,128)S(1)} %pad_maximum_fusion.9), channel_id=1, source_target_pairs={{0,3},{1,0},{2,1},{3,2},{4,7},{5,4},{6,5},{7,6},{8,11},{9,8},{10,9... | collective-permute-start | bytes 147848 | tf_op jit(solution)/shard_map/ppermute | solution.py:47
  34.9 5.7 %copy-start = (f32[128,32,128]{2,1,0:T(8,128)S(1)}, f32[128,32,128]{2,1,0:T(8,128)}, u32[]{:S(2)}) copy-start(f32[128,32,128]{2,1,0:T(8,128)} %param.7) | copy-start | bytes 6291460
  44.3 1.6 %copy-start.3 = (f32[128,32,128]{0,2,1:T(8,128)S(1)}, f32[128,32,128]{0,2,1:T(8,128)}, u32[]{:S(2)}) copy-start(f32[128,32,128]{0,2,1:T(8,128)} %copy.72) | copy-start | bytes 6291460
  47.4 1.6 %copy-start.1 = (f32[128,32,128]{0,2,1:T(8,128)S(1)}, f32[128,32,128]{0,2,1:T(8,128)}, u32[]{:S(2)}) copy-start(f32[128,32,128]{0,2,1:T(8,128)} %copy.89) | copy-start | bytes 6291460
  47.4 2.2 %copy-start.4 = (f32[128,31,128]{0,2,1:T(8,128)S(1)}, f32[128,31,128]{0,2,1:T(8,128)}, u32[]{:S(2)}) copy-start(f32[128,31,128]{0,2,1:T(8,128)} %get-tuple-element.13) | copy-start | bytes 6094852
  47.4 2.8 %copy-start.5 = (f32[128,31,128]{0,2,1:T(8,128)S(1)}, f32[128,31,128]{0,2,1:T(8,128)}, u32[]{:S(2)}) copy-start(f32[128,31,128]{0,2,1:T(8,128)} %get-tuple-element.14) | copy-start | bytes 6094852
  50.2 2.4 %copy-start.8 = (f32[4,256,1]{1,0,2:T(4,128)S(1)}, f32[4,256,1]{1,0,2:T(4,128)}, u32[]{:S(2)}) copy-start(f32[4,256,1]{1,0,2:T(4,128)} %constant.28) | copy-start | bytes 12292
  52.6 13.2 %copy-start.9 = (f32[128,4,1]{0,1,2:T(4,128)S(1)}, f32[128,4,1]{0,1,2:T(4,128)}, u32[]{:S(2)}) copy-start(f32[128,4,1]{0,1,2:T(4,128)} %constant.29) | copy-start | bytes 6148
  54.4 13.2 %copy-start.7 = (f32[128,256,1]{1,0,2:T(8,128)S(1)}, f32[128,256,1]{1,0,2:T(8,128)}, u32[]{:S(2)}) copy-start(f32[128,256,1]{1,0,2:T(8,128)} %constant.27) | copy-start | bytes 393220

commit v2 on v0

v2 whole, which is shorter than its diff:
```python
import functools

import jax
import jax.numpy as jnp
import numpy as np
from jax import lax
from jax.experimental import pallas as pl
from jax.experimental.pallas import tpu as pltpu
from jax.sharding import PartitionSpec as P

coupling = 400.0
LANES = 128
PACK = 32
UNROLL = 4


def constants(m, parts):
    root = (1.0 + 2.0 * coupling - np.sqrt(1.0 + 4.0 * coupling)) / (2.0 * coupling)
    height = 1.0 / (1.0 + 2.0 * coupling - 2.0 * coupling * root)
    step = root**m
    whole = step**parts
    near, far = {}, {}
    for p in range(1, parts + 1):
        near[p] = step ** (p - 1) / (1.0 - whole)
        far[p] = m * step ** (p - 1) * (
            (p - 1) / (1.0 - whole) + parts * whole / (1.0 - whole) ** 2
        )
    return float(root), float(height), near, far


def kernel(
    m, ny, parts, rings,
    f_hbm, c_ref, q_hbm, out_ref,
    fv, qv, hv, av, pf, to_right, to_left, from_left, from_right, d_one, d_two, d_q,
    pieces, gathered, mixed, incoming,
    load_f, load_q, z_send, z_recv, s_one, r_one, s_two, r_two,
):
    groups = m // PACK
    root, height, near, far = constants(m, parts)
    me = lax.axis_index("gy")
    mez = lax.axis_index("gz")
    right = lax.rem(mez + 1, rings)
    left = lax.rem(mez + rings - 1, rings)

    loads = []
    for k in range(groups):
        rows = pl.ds(k * PACK, PACK)
        one = pltpu.make_async_copy(f_hbm.at[rows], fv.at[rows], load_f.at[k])
        two = pltpu.make_async_copy(q_hbm.at[rows], qv.at[rows], load_q.at[k])
        one.start()
        two.start()
        loads.append((one, two))

    barrier = pltpu.get_barrier_semaphore()
    for z in (left, right):
        pl.semaphore_signal(
            barrier, inc=1, device_id={"gz": z}, device_id_type=pl.DeviceIdType.MESH
        )
    for o in range(1, parts):
        pl.semaphore_signal(
            barrier, inc=1, device_id={"gy": lax.rem(me + o, parts)},
            device_id_type=pl.DeviceIdType.MESH,
        )

    c = c_ref[...]
    lane = lax.broadcasted_iota(jnp.int32, (ny, LANES), 1)
    slot = lane % 4
    owner = lane // 4
    zero = jnp.zeros((ny, LANES), jnp.float32)

    def roll(v, by):
        return pltpu.roll(v, by, 1)

    def c_step(j, packed):
        return jnp.where(owner == j, roll(c, 4 * j + 2), packed)

    pc = lax.fori_loop(0, PACK, c_step, zero)
    c_right = roll(pc, 2)
    c_left = roll(pc, LANES - 2)

    sends = []
    for k in range(groups):
        loads[k][0].wait()
        loads[k][1].wait()

        def pack_step(i, carry):
            a, b = carry
            for u in range(UNROLL):
                j = i * UNROLL + u
                hit = owner == j
                a = jnp.where(hit, roll(fv[k * PACK + j], 4 * j + 2), a)
                b = jnp.where(hit, roll(qv[k * PACK + j], 4 * j + 3), b)
            return a, b

        a, b = lax.fori_loop(0, PACK // UNROLL, pack_step, (zero, zero))
        pf[k] = a
        to_right[k] = jnp.where(slot < 2, a, jnp.where(slot == 2, b, c_right))
        to_left[k] = jnp.where(
            slot >= 2, a, jnp.where(slot == 1, roll(b, LANES - 2), c_left)
        )
        if k == 0:
            pl.semaphore_wait(barrier, parts + 1)
        for side, (source, landing, z) in enumerate(
            ((to_right, from_left, right), (to_left, from_right, left))
        ):
            copy = pltpu.make_async_remote_copy(
                src_ref=source.at[k], dst_ref=landing.at[k],
                send_sem=z_send.at[side, k], recv_sem=z_recv.at[side, k],
                device_id={"gz": z}, device_id_type=pl.DeviceIdType.MESH,
            )
            copy.start()
            sends.append(copy)
    for copy in sends:
        copy.wait()

    def across(v):
        return pltpu.roll(v, 1, 0) + pltpu.roll(v, ny - 1, 0)

    c_low = jnp.where(slot < 2, roll(from_left[0], LANES - 2), pc)
    c_high = jnp.where(slot < 2, pc, roll(from_right[0], 2))
    for k in range(groups):
        lo, hi, own = from_left[k], from_right[k], pf[k]

        def update(v, factor):
            return v + factor * (across(v) + roll(v, 1) + roll(v, LANES - 1) - 4.0 * v)

        low = update(jnp.where(slot < 2, lo, own), c_low)
        high = update(jnp.where(slot < 2, own, hi), c_high)
        d_one[k] = jnp.where(slot == 1, roll(hi, LANES - 1), roll(lo, 1))
        d_two[k] = jnp.where(slot == 1, roll(high, LANES - 1), roll(low, 1))
        d_q[k] = jnp.where(slot == 1, hi, lo)

    first = lane == 0
    last = lane == LANES - 1

    def transverse(v, edge):
        below = jnp.where(first, edge, roll(v, 1))
        above = jnp.where(last, edge, roll(v, LANES - 1))
        return v + c * (across(v) + below + above - 4.0 * v)

    carry = zero
    for k in range(groups):
        packed = (d_one[k], d_two[k], d_q[k])

        def forward(i, a):
            for u in range(UNROLL):
                j = i * UNROLL + u
                x = k * PACK + j
                one, two, three = (roll(d, LANES - 2 - 4 * j) for d in packed)
                g = transverse(transverse(fv[x], one), two)
                hv[x] = transverse(qv[x], three)
                fv[x] = g
                a = root * a + g
                av[x] = a
            return a

        carry = lax.fori_loop(0, PACK // UNROLL, forward, carry)
    sum_low = carry

    def backward(i, carry):
        pull, pull_two, ahead, weight = carry
        for u in range(UNROLL):
            x = m - 1 - (i * UNROLL + u)
            b = root * pull
            w = height * (av[x] + b) + hv[x]
            pull = b + fv[x]
            b_two = root * pull_two
            hv[x] = w
            av[x] = b_two
            pull_two = b_two + w
            ahead = ahead + weight * w
            weight = weight * root
        return pull, pull_two, ahead, weight

    sum_high, twice_high, twice_low, _ = lax.fori_loop(
        0, m // UNROLL, backward, (zero, zero, zero, zero + 1.0)
    )
    same = height**2 * root**2 / (1.0 - root**2)
    cross = height**2 * root ** (m + 1) / (1.0 - root**2)
    planes = (
        (height**2 * sum_low, height * twice_low + same * sum_low + cross * sum_high),
        (height**2 * sum_high, height * twice_high + same * sum_high + cross * sum_low),
    )
    half = parts // 2
    rows = ny // half
    for way in range(2):
        for e in range(half):
            for n in range(2):
                pieces[way * half + e, n] = planes[way][n][e * rows : (e + 1) * rows]

    gathered[me] = pieces[me]
    sends = []
    for o in range(1, parts):
        peer = lax.rem(me + o, parts)
        copy = pltpu.make_async_remote_copy(
            src_ref=pieces.at[peer], dst_ref=gathered.at[me],
            send_sem=s_one.at[o], recv_sem=r_one.at[o],
            device_id={"gy": peer}, device_id_type=pl.DeviceIdType.MESH,
        )
        copy.start()
        sends.append(copy)
    for copy in sends:
        copy.wait()

    from_below = me < half
    for d in range(parts):
        total_u = jnp.zeros((rows, LANES), jnp.float32)
        total_v = total_u
        for e in range(parts):
            down = (d - e) % parts or parts
            up = (e - d) % parts or parts
            by = jnp.where(from_below, near[down], near[up])
            by_far = jnp.where(from_below, far[down], far[up])
            total_u = total_u + by * gathered[e, 0]
            total_v = total_v + by * gathered[e, 1] + by_far * gathered[e, 0]
        mixed[d, 0] = total_u
        mixed[d, 1] = total_v

    incoming[me] = mixed[me]
    sends = []
    for o in range(1, parts):
        peer = lax.rem(me + o, parts)
        copy = pltpu.make_async_remote_copy(
            src_ref=mixed.at[peer], dst_ref=incoming.at[me],
            send_sem=s_two.at[o], recv_sem=r_two.at[o],
            device_id={"gy": peer}, device_id_type=pl.DeviceIdType.MESH,
        )
        copy.start()
        sends.append(copy)

    def finish_local(i, a):
        for u in range(UNROLL):
            x = i * UNROLL + u
            a = root * a + hv[x]
            av[x] = height * (a + av[x]) + qv[x]
        return a

    lax.fori_loop(0, m // UNROLL, finish_local, zero)
    for copy in sends:
        copy.wait()

    low_u, low_v, high_u, high_v = (
        jnp.concatenate([incoming[way * half + e, n] for e in range(half)], axis=0)
        for way in range(2)
        for n in range(2)
    )
    mirror = height**2 * root / (1.0 - root**2)
    low_v = low_v + mirror * sum_high
    high_v = high_v + mirror * sum_low

    def add_high(i, carry):
        u_now, v_now = carry
        for u in range(UNROLL):
            x = m - 1 - (i * UNROLL + u)
            u_now = root * u_now
            v_now = root * v_now + u_now
            av[x] = av[x] + v_now
        return u_now, v_now

    lax.fori_loop(0, m // UNROLL, add_high, (high_u, high_v))

    def add_low(i, carry):
        u_now, v_now = carry
        for u in range(UNROLL):
            x = i * UNROLL + u
            u_now = root * u_now
            v_now = root * v_now + u_now
            out_ref[x] = av[x] + v_now
        return u_now, v_now

    lax.fori_loop(0, m // UNROLL, add_low, (low_u, low_v))


def per_device(field, c, q):
    m, ny, nz = field.shape
    parts = lax.axis_size("gy")
    rings = lax.axis_size("gz")
    assert nz == LANES and m % PACK == 0 and ny % (parts // 2) == 0
    groups = m // PACK
    rows = ny // (parts // 2)
    block = pltpu.VMEM((m, ny, nz), jnp.float32)
    packed = pltpu.VMEM((groups, ny, LANES), jnp.float32)
    small = pltpu.VMEM((parts, 2, rows, LANES), jnp.float32)
    dma = pltpu.SemaphoreType.DMA
    return pl.pallas_call(
        functools.partial(kernel, m, ny, parts, rings),
        out_shape=jax.ShapeDtypeStruct(field.shape, jnp.float32),
        in_specs=[
            pl.BlockSpec(memory_space=pltpu.HBM),
            pl.BlockSpec(memory_space=pltpu.VMEM),
            pl.BlockSpec(memory_space=pltpu.HBM),
        ],
        out_specs=pl.BlockSpec(memory_space=pltpu.VMEM),
        scratch_shapes=[block] * 4 + [packed] * 8 + [small] * 4 + [
            dma((groups,)), dma((groups,)), dma((2, groups)), dma((2, groups)),
            dma((parts,)), dma((parts,)), dma((parts,)), dma((parts,)),
        ],
        compiler_params=pltpu.CompilerParams(
            collective_id=0, has_side_effects=True, vmem_limit_bytes=28 * 2**20
        ),
    )(field, c, q)


def solution(mesh):
    placed = (P("gy", None, "gz"), P(None, "gz"), P("gy", None, "gz"))
    return jax.shard_map(
        per_device, mesh=mesh, in_specs=placed, out_specs=P("gy", None, "gz"), check_vma=False
    )
```

time: 154 us -> 38 us (0.25)
  waiting for transfers between devices: 60.4 us -> 0 us
  Pallas kernels: 0 us -> 32.5 us
  blocking collectives: 29.1 us -> 0 us
  starting transfers between devices: 20.4 us -> 0 us
  local copies, waits for them, and re-layouts: 23.7 us -> 5.22 us
  matrix products: 13.6 us -> 0 us
  other arithmetic: 6.27 us -> 0 us
    ppermute x8 -> x0, waiting for transfers between devices: 37.9 us -> none  [the longest x4 31.3 us: with_halo(): lax.ppermute(lax.slice_in_dim(block, 0, width, axis=dim), axis, backward)]
    pallas_call x0 -> x1, Pallas kernels: none -> 32.5 us  [per_device(): pl.pallas_call(functools.partial(kernel, m, ny, parts, rings), out_shape=...]
    all_to_all x1 -> x0, blocking collectives: 29.1 us -> none  [per_device(): return lax.all_to_all(lines, 'gy', split_axis=0, concat_axis=1, tiled=True)]
    all_to_all x2 -> x0, waiting for transfers between devices: 22.5 us -> none  [the longest x1 22.5 us: per_device(): lax.all_to_all(initial_warmth, 'gy', split_axis=1, concat_axis=0, tiled=T...]
    dot_general x2 -> x0, matrix products: 13.6 us -> none  [solve_lines(): jnp.dot(table, flat, precision=lax.Precision.HIGHEST, preferred_element_t...]
    ppermute x8 -> x0, starting transfers between devices: 10.9 us -> none  [the longest x4 8.8 us: with_halo(): lax.ppermute(lax.slice_in_dim(block, 0, width, axis=dim), axis, backward)]
    all_to_all x2 -> x0, starting transfers between devices: 9.54 us -> none  [the longest x1 5.2 us: per_device(): lax.all_to_all(initial_warmth, 'gy', split_axis=1, concat_axis=0, tiled=T...]
    all_to_all x4 -> x0, local copies, waits for them, and re-layouts: 9.38 us -> none  [the longest x2 5.62 us: per_device(): lax.all_to_all(energy_supply_series, 'gy', split_axis=1, concat_axis=0, t...]
  transfers between devices with their start and end apart: 10 -> 0, of which waited for: 6 -> 0; matrix products, arithmetic and copies ran while one was open for 12% -> 0% of each run, Pallas kernels for 0% -> 0%
where the time goes in v2:
time: 38 us; the launch traced here: 37.7 us
  Pallas kernels  32.5 us (86%)
  local copies, waits for them, and re-layouts  5.22 us (14%)
    pallas_call x1, Pallas kernels, per_device(): pl.pallas_call(functools.partial(kernel, m, ny, parts, rings), out_shape=...  32.5 us
    unnamed x7, local copies, waits for them, and re-layouts  5.22 us

profile of v2, /device:TPU:0, one launch (start us, length us, event | category | flops | bytes accessed | tf_op | source)
XLA Modules:
  0.0 37.7 jit_solution(77416549567046886)
XLA Ops:
  0.0 0.0 copy-start
  0.0 1.6 %copy-done = f32[128,32,128]{2,1,0:T(8,128)S(1)} copy-done((f32[128,32,128]{2,1,0:T(8,128)S(1)}, f32[128,32,128]{2,1,0:T(8,128)}, u32[]{:S(2)}) %copy-start) | copy-done | bytes 2097176
  1.6 0.0 copy-start.1
  1.6 1.6 %copy-done.1 = f32[128,32,128]{2,1,0:T(8,128)S(1)} copy-done((f32[128,32,128]{2,1,0:T(8,128)S(1)}, f32[128,32,128]{2,1,0:T(8,128)}, u32[]{:S(2)}) %copy-start.1) | copy-done | bytes 2097176
  3.2 0.0 copy-start.2
  3.2 0.7 %copy-done.2 = f32[32,128]{1,0:T(8,128)S(1)} copy-done((f32[32,128]{1,0:T(8,128)S(1)}, f32[32,128]{1,0:T(8,128)}, u32[]{:S(2)}) %copy-start.2) | copy-done | bytes 16408
  3.9 32.5 %shard_map.37 = f32[128,32,128]{2,1,0:T(8,128)S(1)} custom-call(f32[128,32,128]{2,1,0:T(8,128)S(1)} %copy-done, f32[32,128]{1,0:T(8,128)S(1)} %copy-done.2, f32[128,32,128]{2,1,0:T(8,128)S(1)} %copy-done.1), custom_call_target="tpu_custom_call" | custom-call | tf_op jit(solution)/shard_map/pallas_call | solution.py:285
  36.4 1.3 %copy.5 = f32[128,32,128]{2,1,0:T(8,128)} copy(f32[128,32,128]{2,1,0:T(8,128)S(1)} %shard_map.37) | data formatting | bytes 4194304
Async XLA Ops:
  0.0 1.6 %copy-start = (f32[128,32,128]{2,1,0:T(8,128)S(1)}, f32[128,32,128]{2,1,0:T(8,128)}, u32[]{:S(2)}) copy-start(f32[128,32,128]{2,1,0:T(8,128)} %f_hbm.1) | copy-start | bytes 6291460
  1.6 1.6 %copy-start.1 = (f32[128,32,128]{2,1,0:T(8,128)S(1)}, f32[128,32,128]{2,1,0:T(8,128)}, u32[]{:S(2)}) copy-start(f32[128,32,128]{2,1,0:T(8,128)} %q_hbm.1) | copy-start | bytes 6291460
  3.2 0.7 %copy-start.2 = (f32[32,128]{1,0:T(8,128)S(1)}, f32[32,128]{1,0:T(8,128)}, u32[]{:S(2)}) copy-start(f32[32,128]{1,0:T(8,128)} %c_ref.1) | copy-start | bytes 49156

commit v3 on v2

--- a/solution.py
+++ b/solution.py
@@ -298,7 +298,7 @@
         compiler_params=pltpu.CompilerParams(
             collective_id=0, has_side_effects=True, vmem_limit_bytes=28 * 2**20
         ),
-    )(field, c, q)
+    )(pltpu.with_memory_space_constraint(field, pltpu.HBM), c, pltpu.with_memory_space_constraint(q, pltpu.HBM))
 
 
 def solution(mesh):

time: 38 us -> 34.4 us (0.905)
  local copies, waits for them, and re-layouts: 5.22 us -> 2.04 us
  Pallas kernels: 32.5 us -> 32.1 us
    unnamed x7 -> x3, local copies, waits for them, and re-layouts: 5.22 us -> 2.04 us
where the time goes in v3:
time: 34.4 us; the launch traced here: 34.2 us
  Pallas kernels  32.1 us (93%)
  local copies, waits for them, and re-layouts  2.04 us (6%)
    pallas_call x1, Pallas kernels, per_device(): pl.pallas_call(functools.partial(kernel, m, ny, parts, rings), out_shape=...  32.1 us
    unnamed x3, local copies, waits for them, and re-layouts  2.04 us

profile of v3, /device:TPU:0, one launch (start us, length us, event | category | flops | bytes accessed | tf_op | source)
XLA Modules:
  0.0 34.2 jit_solution(5876427282234891149)
XLA Ops:
  0.0 0.0 copy-start
  0.0 0.7 %copy-done = f32[32,128]{1,0:T(8,128)S(1)} copy-done((f32[32,128]{1,0:T(8,128)S(1)}, f32[32,128]{1,0:T(8,128)}, u32[]{:S(2)}) %copy-start) | copy-done | bytes 16408
  0.7 32.1 %shard_map.37 = f32[128,32,128]{2,1,0:T(8,128)S(1)} custom-call(f32[128,32,128]{2,1,0:T(8,128)} %f_hbm.1, f32[32,128]{1,0:T(8,128)S(1)} %copy-done, f32[128,32,128]{2,1,0:T(8,128)} %q_hbm.1), custom_call_target="tpu_custom_call" | custom-call | tf_op jit(solution)/shard_map/pallas_call | solution.py:285
  32.9 1.3 %copy.5 = f32[128,32,128]{2,1,0:T(8,128)} copy(f32[128,32,128]{2,1,0:T(8,128)S(1)} %shard_map.37) | data formatting | bytes 4194304
Async XLA Ops:
  0.0 0.7 %copy-start = (f32[32,128]{1,0:T(8,128)S(1)}, f32[32,128]{1,0:T(8,128)}, u32[]{:S(2)}) copy-start(f32[32,128]{1,0:T(8,128)} %c_ref.1) | copy-start | bytes 49156

commit v4 on v3

--- a/solution.py
+++ b/solution.py
@@ -85,14 +85,14 @@
 
         def pack_step(i, carry):
             a, b = carry
-            for u in range(UNROLL):
-                j = i * UNROLL + u
+            for u in range(2 * UNROLL):
+                j = i * 2 * UNROLL + u
                 hit = owner == j
                 a = jnp.where(hit, roll(fv[k * PACK + j], 4 * j + 2), a)
                 b = jnp.where(hit, roll(qv[k * PACK + j], 4 * j + 3), b)
             return a, b
 
-        a, b = lax.fori_loop(0, PACK // UNROLL, pack_step, (zero, zero))
+        a, b = lax.fori_loop(0, PACK // (2 * UNROLL), pack_step, (zero, zero))
         pf[k] = a
         to_right[k] = jnp.where(slot < 2, a, jnp.where(slot == 2, b, c_right))
         to_left[k] = jnp.where(
@@ -110,15 +110,35 @@
             )
             copy.start()
             sends.append(copy)
-    for copy in sends:
-        copy.wait()
+    first = lane == 0
+    last = lane == LANES - 1
+    stay = 1.0 - 4.0 * c
+    c_edge = jnp.where(first | last, c, 0.0)
 
     def across(v):
         return pltpu.roll(v, 1, 0) + pltpu.roll(v, ny - 1, 0)
 
-    c_low = jnp.where(slot < 2, roll(from_left[0], LANES - 2), pc)
-    c_high = jnp.where(slot < 2, pc, roll(from_right[0], 2))
+    def transverse(v, edge):
+        below = jnp.where(first, edge, roll(v, 1))
+        above = jnp.where(last, edge, roll(v, LANES - 1))
+        return stay * v + c * (across(v) + below + above)
+
+    def inner(i, carry):
+        for u in range(UNROLL):
+            x = i * UNROLL + u
+            fv[x] = transverse(fv[x], 0.0)
+            hv[x] = transverse(qv[x], 0.0)
+        return carry
+
+    lax.fori_loop(0, m // UNROLL, inner, 0)
+
+    carry = zero
     for k in range(groups):
+        sends[2 * k].wait()
+        sends[2 * k + 1].wait()
+        if k == 0:
+            c_low = jnp.where(slot < 2, roll(from_left[0], LANES - 2), pc)
+            c_high = jnp.where(slot < 2, pc, roll(from_right[0], 2))
         lo, hi, own = from_left[k], from_right[k], pf[k]
 
         def update(v, factor):
@@ -130,25 +150,15 @@
         d_two[k] = jnp.where(slot == 1, roll(high, LANES - 1), roll(low, 1))
         d_q[k] = jnp.where(slot == 1, hi, lo)
 
-    first = lane == 0
-    last = lane == LANES - 1
-
-    def transverse(v, edge):
-        below = jnp.where(first, edge, roll(v, 1))
-        above = jnp.where(last, edge, roll(v, LANES - 1))
-        return v + c * (across(v) + below + above - 4.0 * v)
-
-    carry = zero
-    for k in range(groups):
-        packed = (d_one[k], d_two[k], d_q[k])
-
         def forward(i, a):
             for u in range(UNROLL):
                 j = i * UNROLL + u
                 x = k * PACK + j
-                one, two, three = (roll(d, LANES - 2 - 4 * j) for d in packed)
-                g = transverse(transverse(fv[x], one), two)
-                hv[x] = transverse(qv[x], three)
+                back = LANES - 2 - 4 * j
+                g = transverse(
+                    fv[x] + c_edge * roll(d_one[k], back), roll(d_two[k], back)
+                )
+                hv[x] = hv[x] + c_edge * roll(d_q[k], back)
                 fv[x] = g
                 a = root * a + g
                 av[x] = a

time: 34.4 us -> 29.3 us (0.85)
  Pallas kernels: 32.1 us -> 27 us
    pallas_call x1, Pallas kernels: 32.1 us -> 27 us  [per_device(): pl.pallas_call(functools.partial(kernel, m, ny, parts, rings), out_shape=...]
where the time goes in v4:
time: 29.3 us; the launch traced here: 29.1 us
  Pallas kernels  27 us (92%)
  local copies, waits for them, and re-layouts  2.04 us (7%)
    pallas_call x1, Pallas kernels, per_device(): pl.pallas_call(functools.partial(kernel, m, ny, parts, rings), out_shape=...  27 us
    unnamed x3, local copies, waits for them, and re-layouts  2.04 us

profile of v4, /device:TPU:0, one launch (start us, length us, event | category | flops | bytes accessed | tf_op | source)
XLA Modules:
  0.0 29.1 jit_solution(10235952230929150645)
XLA Ops:
  0.0 0.0 copy-start
  0.0 0.7 %copy-done = f32[32,128]{1,0:T(8,128)S(1)} copy-done((f32[32,128]{1,0:T(8,128)S(1)}, f32[32,128]{1,0:T(8,128)}, u32[]{:S(2)}) %copy-start) | copy-done | bytes 16408
  0.7 27.0 %shard_map.37 = f32[128,32,128]{2,1,0:T(8,128)S(1)} custom-call(f32[128,32,128]{2,1,0:T(8,128)} %f_hbm.1, f32[32,128]{1,0:T(8,128)S(1)} %copy-done, f32[128,32,128]{2,1,0:T(8,128)} %q_hbm.1), custom_call_target="tpu_custom_call" | custom-call | tf_op jit(solution)/shard_map/pallas_call | solution.py:295
  27.7 1.3 %copy.5 = f32[128,32,128]{2,1,0:T(8,128)} copy(f32[128,32,128]{2,1,0:T(8,128)S(1)} %shard_map.37) | data formatting | bytes 4194304
Async XLA Ops:
  0.0 0.7 %copy-start = (f32[32,128]{1,0:T(8,128)S(1)}, f32[32,128]{1,0:T(8,128)}, u32[]{:S(2)}) copy-start(f32[32,128]{1,0:T(8,128)} %c_ref.1) | copy-start | bytes 49156
